TPU v7x, 32 devices: a whole 2x2x4 slice. The times are simulated.
32 devices in a mesh: grp: 4 (over y, x), side: 2 (over core), seq: 4 (over z).
Axes of the slice: x: 2, y: 2, z: 4, core: 2. Of those that a mesh axis runs over, the one named last changes fastest.
Arguments:
- queries: bfloat16 [2, 4, 256, 64, 576], P('side', 'grp', 'seq'), may hold values from -48 to 48
- stream_rows: bfloat16 [2, 4, 256, 576], P('side', 'grp', 'seq'), may hold values from -6 to 6
- span_latents: bfloat16 [4, 256, 576], P('grp', 'seq'), may hold values from -6 to 6
- decode_cache: bfloat16 [65536, 576], P(('grp', 'seq')), may hold values from -6 to 6
- cache_lengths: int32 [16, 64], P(('grp', 'seq')), may hold values from 1 to 256, 4096 in all within a row
- block_owner: int32 [32, 1], replicated, may hold values from 0 to 15; in each aligned block of 32 rows (0 to 31, 32 to 63, ...) at most 4 rows name the same one
- block_request: int32 [32], replicated, may hold values from 0 to 63
Outputs:
- attended: bfloat16 [2, 4, 256, 64, 512], P('side', 'grp', 'seq')
Inputs may be any that keep to these rules, and one draw needn't show every extreme that they name: Each row of cache_lengths sums to 4096; a device's requests take consecutive rows of its 4096 resident rows in order. `block_owner`: decode devices are numbered grp index * 4 + seq index; no device receives more than 4 blocks.
All inputs are finite; a program needn't handle non-finite values.
Results may differ from a plain program's by a relative error of at most 0.0048.
Values may be sent and summed in bfloat16 or wider, within the bound.
No kernel may reach another device: no remote copies, remote signals or barrier semaphores. Data moves between devices by JAX's collectives and lax.ppermute only.
A program may use at most 128 MiB of HBM per device.

v0:
```python
import math
import jax
import jax.numpy as jnp
from jax import lax
from jax.sharding import PartitionSpec as P

LAT = 512
ROPE = 64
NOPE = 128
BLOCK = 32
MOSTLEN = 256


def shifted(block, axis, distance):
    devices = range(lax.axis_size(axis))
    route = [(i - distance, i) for i in devices if i - distance in devices]
    return lax.ppermute(block, axis, route)


def masked_weights(score_rows, allowed):
    masked = jnp.where(allowed, score_rows, -jnp.inf)
    largest = jnp.max(masked, axis=-1, keepdims=True)
    lifted = jnp.exp(masked - largest)
    return (lifted / jnp.sum(lifted, axis=-1, keepdims=True)).astype(jnp.bfloat16)


def prefill_side(own_query, key_rows, first_row):
    row_count, head_count, row_width = own_query.shape
    span_rows = key_rows.shape[0] // 2
    factor = 1.0 / math.sqrt(NOPE + ROPE)
    head_group = min(head_count, max(1, 512 // row_count))
    allowed = (jnp.arange(2 * span_rows) - span_rows)[None, None, :] <= (
        first_row + jnp.arange(row_count)
    )[:, None, None]
    grouped = jnp.transpose(
        own_query.reshape(row_count, head_count // head_group, head_group, row_width), (1, 0, 2, 3)
    )
    value_rows = key_rows[:, :LAT]

    def one_group(group_query):
        scored = (
            jnp.einsum("rhw,kw->rhk", group_query, key_rows, preferred_element_type=jnp.float32)
            * factor
        )
        weights = masked_weights(scored, allowed)
        return jnp.einsum(
            "rhk,kl->rhl", weights, value_rows, preferred_element_type=jnp.float32
        ).astype(jnp.bfloat16)

    results = lax.map(one_group, grouped)
    return jnp.transpose(results, (1, 0, 2, 3)).reshape(row_count, head_count, LAT)


def decode_side(own_query, own_latent, pool_rows, lengths, arrived, arrived_allowed):
    row_count = own_query.shape[0]
    factor = 1.0 / math.sqrt(NOPE + ROPE)
    offsets = jnp.cumsum(lengths) - lengths
    padded = jnp.concatenate(
        [pool_rows, jnp.zeros((MOSTLEN, pool_rows.shape[1]), pool_rows.dtype)], 0
    )
    row_index = offsets[:, None] + jnp.arange(MOSTLEN, dtype=jnp.int32)[None, :]
    windows = jnp.take(padded, row_index, axis=0)
    resident = (
        jnp.einsum("rhw,rtw->rht", own_query, windows, preferred_element_type=jnp.float32) * factor
    )
    incoming = (
        jnp.einsum("rhw,kw->rhk", own_query, arrived, preferred_element_type=jnp.float32) * factor
    )
    itself = (
        jnp.einsum("rhw,rw->rh", own_query, own_latent, preferred_element_type=jnp.float32)[
            :, :, None
        ]
        * factor
    )
    scored = jnp.concatenate([resident, incoming, itself], -1)
    resident_allowed = jnp.arange(MOSTLEN)[None, :] < lengths[:, None]
    allowed = jnp.concatenate(
        [resident_allowed, arrived_allowed, jnp.ones((row_count, 1), jnp.bool_)], -1
    )[:, None, :]
    weights = masked_weights(scored, allowed)
    split_point = MOSTLEN + arrived.shape[0]
    context = jnp.einsum(
        "rht,rtl->rhl",
        weights[:, :, :MOSTLEN],
        windows[:, :, :LAT],
        preferred_element_type=jnp.float32,
    )
    context = context + jnp.einsum(
        "rhk,kl->rhl",
        weights[:, :, MOSTLEN:split_point],
        arrived[:, :LAT],
        preferred_element_type=jnp.float32,
    )
    context = context + weights[:, :, split_point:].astype(jnp.float32) * own_latent[
        :, None, :LAT
    ].astype(jnp.float32)
    return context.astype(jnp.bfloat16)


def local(
    queries, stream_rows, span_latents, decode_cache, cache_lengths, block_owner, block_request
):
    own_query = queries[0, 0]
    own_stream = stream_rows[0, 0]
    own_span = span_latents[0]
    row_count = own_query.shape[0]
    row_width = own_stream.shape[1]
    seq_index = lax.axis_index("seq")
    grp_index = lax.axis_index("grp")
    side_index = lax.axis_index("side")
    seq_count = lax.axis_size("seq")
    per_device = row_count // BLOCK
    capacity = 2 * per_device
    owners = block_owner[:, 0]
    total_blocks = owners.shape[0]
    my_owner = grp_index * seq_count + seq_index
    earlier, current = (
        lax.all_gather(own_stream, "seq", axis=0, tiled=True),
        lax.all_gather(own_span, "seq", axis=0, tiled=True),
    )
    handed = shifted(own_stream, "side", 1)
    landed = lax.all_gather(handed, ("grp", "seq"), axis=0, tiled=True)
    landed = landed.reshape(total_blocks, BLOCK, row_width)
    block_ids = jnp.arange(total_blocks, dtype=jnp.int32)
    order_key = jnp.where(owners == my_owner, block_ids, total_blocks + block_ids)
    picked = jnp.argsort(order_key)[:capacity]
    present = owners[picked] == my_owner
    requests = block_request[picked]
    arrived = landed[picked].reshape(capacity * BLOCK, row_width)
    arrived_allowed = jnp.repeat(
        present[None, :] & (requests[None, :] == jnp.arange(row_count)[:, None]), BLOCK, axis=1
    )
    first_row = seq_index * row_count
    key_rows = jnp.concatenate([earlier, current], 0)
    context = lax.cond(
        side_index == 0,
        lambda: prefill_side(own_query, key_rows, first_row),
        lambda: decode_side(
            own_query, own_stream, decode_cache, cache_lengths[0], arrived, arrived_allowed
        ),
    )
    return context[None, None]


def solution(mesh):
    return jax.shard_map(
        local,
        mesh=mesh,
        in_specs=(
            P("side", "grp", "seq", None, None),
            P("side", "grp", "seq", None),
            P("grp", "seq", None),
            P(("grp", "seq"), None),
            P(("grp", "seq"), None),
            P(),
            P(),
        ),
        out_specs=P("side", "grp", "seq", None, None),
        check_vma=False,
    )
```

profile of v0, /device:TPU:1, one launch (start us, length us, event | category | flops | bytes accessed | tf_op | source)
XLA Modules:
  0.0 228.1 jit_solution(6818129309431499111)
XLA Ops:
  6.5 1.3 collective-permute-start
  7.8 2.1 collective-permute-done
  10.6 0.7 compare_select_fusion.3
  11.2 1.7 sort.17
  12.9 14.4 %all-gather = bf16[1,1,256,576]{3,2,1,0:T(8,128)(2,1)S(1)} all-gather(bf16[1,1,64,576]{3,2,1,0:T(8,128)(2,1)} %param.12), channel_id=2, replica_groups=mesh['grp'=4,'side'=2,'seq'=4] {'seq'}, dimensions={2}, use_global_device_ids=true | all-gather | bytes 368640 | tf_op jit(solution)/shard_map/all_gather | solution.py:118
  27.3 11.7 %all-gather.1 = bf16[1,256,576]{2,1,0:T(8,128)(2,1)S(1)} all-gather(bf16[1,64,576]{2,1,0:T(8,128)(2,1)} %param.13), channel_id=3, replica_groups=mesh['grp'=4,'side'=2,'seq'=4] {'seq'}, dimensions={1}, use_global_device_ids=true | all-gather | bytes 368640 | tf_op jit(solution)/shard_map/all_gather | solution.py:119
  39.0 28.3 %all-gather.4.cloned.1.call-done = bf16[1024,576]{1,0:T(8,128)(2,1)} async-done(((bf16[64,576]{1,0:T(8,128)(2,1)}), bf16[1024,576]{1,0:T(8,128)(2,1)}) %all-gather.4.cloned.1.call-update) | async-done | bytes 1179664 | tf_op jit(solution)/shard_map/all_gather | solution.py:122
  67.4 151.9 %conditional.1 = (bf16[1,1,64,64,512]{4,3,2,1,0:T(8,128)(2,1)S(1)}) conditional(s32[]{:T(128)} %convert_element_type.20, (s32[1,64]{1,0:T(1,128)}, s32[32]{0:T(128)}, bf16[4096,576]{0,1:T(8,128)(2,1)}, bf16[1,1,64,64,576]{4,3,2,1,0:T(8,128)(2,1)}, bf16[1024,576]{1,0:T(8,128)(2,1)}, /*index=5*/bf16[64,576]{1,0:T(8,128)(2,1)}, ...), branch_computations={%region_1.5_spmd.clone, %region_5.10_spmd} | conditional | flops 3458017280 | bytes 214683328 | solution.py:135
  67.4 0.7 copy.48
  68.3 0.7 bitcast_subtract_fusion
  69.1 7.7 %copy.55 = bf16[4096,576]{1,0:T(8,128)(2,1)} copy(bf16[4096,576]{0,1:T(8,128)(2,1)} %get-tuple-element.198) | data formatting | bytes 9437184 | tf_op jit(solution)/shard_map
  76.8 5.4 %concatenate.14 = bf16[4352,576]{1,0:T(8,128)(2,1)} pad(bf16[4096,576]{1,0:T(8,128)(2,1)} %copy.55, bf16[]{:T(256)} %constant.39.clone.1), padding=0_256x0_0 | pad | bytes 9732098 | tf_op jit(solution)/shard_map/cond/branch_0_fun/concatenate | solution.py:58
  82.1 72.1 %gather_fusion = bf16[16384,576]{1,0:T(8,128)(2,1)} fusion(bf16[4352,576]{1,0:T(8,128)(2,1)} %concatenate.14, s32[16384]{0:T(1024)S(1)} %broadcast_clamp_fusion), kind=kCustom, calls=%fused_computation | custom fusion | bytes 37814272 | tf_op jit(solution)/shard_map/cond/branch_0_fun/jit(_take)/gather | solution.py:62
  154.3 18.1 %broadcast_select_fusion = bf16[64,256,576]{2,1,0:T(8,128)(2,1)} fusion(bf16[64,256,576]{2,1,0:T(8,128)(2,1)} %bitcast.97, pred[64,256]{1,0:T(8,128)(4,1)S(1)} %fusion.50), kind=kLoop, calls=%fused_computation.29 | loop fusion | flops 9437184 | bytes 37765120 | tf_op jit(solution)/shard_map/cond/branch_0_fun/jit(_take)/select_n | solution.py:62
  172.4 13.1 %multiply_bitcast_fusion = f32[64,64,256]{2,1,0:T(8,128)} fusion(bf16[64,256,576]{2,1,0:T(8,128)(2,1)} %broadcast_select_fusion, bf16[1,1,64,64,576]{4,3,2,1,0:T(8,128)(2,1)} %get-tuple-element.106), kind=kOutput, calls=%fused_computation.45 | convolution fusion | flops 1209008128 | bytes 27787264 | tf_op jit(solution)/shard_map/cond/branch_0_fun/rhw,rtw->rht/dot_general | solution.py:64
  187.2 2.0 gather_fusion.1
  189.2 4.2 %multiply_bitcast_fusion.1 = f32[64,64,128]{2,1,0:T(8,128)S(1)} fusion(bf16[128,576,1]{1,0,2:T(8,128)(2,1)S(1)} %bitcast.103, bf16[1,1,64,64,576]{4,3,2,1,0:T(8,128)(2,1)} %get-tuple-element.106), kind=kOutput, calls=%fused_computation.49 | convolution fusion | flops 604504064 | bytes 6963200 | tf_op jit(solution)/shard_map/cond/branch_0_fun/rhw,kw->rhk/dot_general | solution.py:67
  193.4 1.7 fusion.30
  195.1 2.0 copy.51
  197.2 4.3 %fusion.58 = (f32[64,64]{1,0:T(8,128)S(1)}, f32[64,64,385]{2,1,0:T(8,128)S(1)}) fusion(f32[64,64,1]{2,1,0:T(8,128)} %copy.51, f32[64,64,128]{2,1,0:T(8,128)S(1)} %multiply_bitcast_fusion.1, f32[64,64,256]{2,1,0:T(8,128)} %multiply_bitcast_fusion, pred[64,385]{1,0:T(8,128)(4,1)S(1)} %add_add_fusion), kind=kOutput, calls=%fused_computation.74 | output fusion | flops 7885184 | bytes 12656704 | tf_op jit(solution)/shard_map/cond/branch_0_fun/sub | solution.py:23
  201.5 0.8 divide_convert_fusion.2
  202.3 12.1 %fusion.28 = f32[64,64,512]{2,1,0:T(8,128)} fusion(bf16[64,256,576]{2,1,0:T(8,128)(2,1)} %broadcast_select_fusion, bf16[64,64,385]{2,1,0:T(8,128)(2,1)S(1)} %divide_convert_fusion.2), kind=kOutput, calls=%fused_computation.30 | convolution fusion | flops 1073741824 | bytes 27262976 | tf_op jit(solution)/shard_map/cond/branch_0_fun/rht,rtl->rhl/dot_general | solution.py:82
  215.1 4.2 %fusion.37 = bf16[1,1,64,64,512]{4,3,2,1,0:T(8,128)(2,1)S(1)} fusion(f32[64,64,512]{2,1,0:T(8,128)} %fusion.28, f32[64,512]{1,0:T(8,128)S(1)} %slice_convert_fusion, f32[64,64]{1,0:T(8,128)S(1)} %convert_reduce_fusion, bf16[64,64,385]{2,1,0:T(8,128)(2,1)S(1)} %divide_convert_fusion.2, bf16[128,576]{1,0:T(8,128)(2,1)S(1)} %bitcast.104), kind=kOutput, calls=%fused_computation.43 | convolution fusion | flops 545259520 | bytes 13926400 | tf_op jit(solution)/shard_map/cond/branch_0_fun/rhk,kl->rhl/dot_general | solution.py:88
  219.3 2.0 copy-done.2
  (41 shorter events, 3.4 us)
Async XLA Ops:
  6.5 60.8 %all-gather.4.cloned.1.call-start = ((), (), s32[]{:S(2)}) async-start(), calls=%async_computation | async-start | bytes 1392640 | tf_op jit(solution)/shard_map/all_gather | solution.py:122
  6.5 3.4 %collective-permute-start = (bf16[64,576]{1,0:T(8,128)(2,1)}, bf16[64,576]{1,0:T(8,128)(2,1)S(1)}, u32[]{:S(2)}, u32[]{:S(2)}) collective-permute-start(bf16[64,576]{1,0:T(8,128)(2,1)} %bitcast.105), channel_id=1, source_target_pairs={{0,4},{1,5},{2,6},{3,7},{8,12},{9,13},{10,14},{11,15},{16,20},{17,... | collective-permute-start | bytes 221192 | tf_op jit(solution)/shard_map/ppermute | solution.py:17
  9.9 0.6 copy-start.4
  172.4 13.1 %copy-start = (s32[32]{0:T(128)S(1)}, s32[32]{0:T(128)}, u32[]{:S(2)}) copy-start(s32[32]{0:T(128)} %get-tuple-element.112) | copy-start | bytes 388 | tf_op jit(solution)/shard_map/cond
  172.4 13.8 %copy-start.1 = (s32[32]{0:T(128)S(1)}, s32[32]{0:T(128)}, u32[]{:S(2)}) copy-start(s32[32]{0:T(128)} %get-tuple-element.116) | copy-start | bytes 388 | tf_op jit(solution)/shard_map/cond
  172.4 14.6 %copy-start.5 = (s32[1,64]{1,0:T(1,128)S(1)}, s32[1,64]{1,0:T(1,128)}, u32[]{:S(2)}) copy-start(s32[1,64]{1,0:T(1,128)} %get-tuple-element.107) | copy-start | bytes 772 | tf_op jit(solution)/shard_map/cond
  186.9 6.4 %slice-start = ((s8[5242880]{0:T(1024)(128)(4,1)}), s8[1048576]{0:T(1024)(128)(4,1)S(1)}, s32[]{:S(2)}) async-start(s8[5242880]{0:T(1024)(128)(4,1)} %bitcast.98), calls=%async_computation.1 | async-start | bytes 2097152 | tf_op jit(solution)/shard_map/cond
  186.9 6.4 %copy-start.3 = (bf16[64,576]{1,0:T(8,128)(2,1)S(1)}, bf16[64,576]{1,0:T(8,128)(2,1)}, u32[]{:S(2)}) copy-start(bf16[64,576]{1,0:T(8,128)(2,1)} %get-tuple-element.105) | copy-start | bytes 221188 | tf_op jit(solution)/shard_map/cond
  189.2 4.2 %slice-start.1 = ((s8[5242880]{0:T(1024)(128)(4,1)}), s8[4194304]{0:T(1024)(128)(4,1)S(1)}, s32[]{:S(2)}) async-start(s8[5242880]{0:T(1024)(128)(4,1)} %bitcast.98), calls=%async_computation.2 | async-start | bytes 8388608 | tf_op jit(solution)/shard_map/cond
  219.3 2.0 copy-start.2
Sparse Core Ops, SparseCore 0:
  10.7 56.6 all-gather.3
where the time goes:
time: 229 us; the launch traced here: 228 us
  local copies, waits for them, and re-layouts  94 us (41%)
  matrix products  35.3 us (15%)
  waiting for transfers between devices  30.4 us (13%)
  other arithmetic  27.5 us (12%)
  blocking collectives  26 us (11%)
  between operations  13.4 us (6%)
    gather x1, local copies, waits for them, and re-layouts, decode_side(): windows = jnp.take(padded, row_index, axis=0)  72.1 us
    all_gather x1, waiting for transfers between devices, local(): landed = lax.all_gather(handed, ('grp', 'seq'), axis=0, tiled=True)  28.3 us
    select_n x1, other arithmetic, decode_side(): windows = jnp.take(padded, row_index, axis=0)  18.1 us
    all_gather x1, blocking collectives, local(): lax.all_gather(own_stream, 'seq', axis=0, tiled=True)  14.4 us
    dot_general x1, matrix products, decode_side(): jnp.einsum('rhw,rtw->rht', own_query, windows, preferred_element_type=jnp...  13.1 us
    dot_general x1, matrix products, decode_side(): jnp.einsum('rht,rtl->rhl', weights[:, :, :MOSTLEN], windows[:, :, :LAT],...  12.1 us
    all_gather x1, blocking collectives, local(): lax.all_gather(own_span, 'seq', axis=0, tiled=True)  11.7 us
    another operation x2, local copies, waits for them, and re-layouts  8.39 us
  transfers between devices with their start and end apart: 2, of which 2 were waited for; matrix products, arithmetic and copies ran while one was open for 1% of the time, Pallas kernels for 0%

commit v1 on v0

--- a/solution.py
+++ b/solution.py
@@ -119,7 +119,32 @@
         lax.all_gather(own_span, "seq", axis=0, tiled=True),
     )
     handed = shifted(own_stream, "side", 1)
-    landed = lax.all_gather(handed, ("grp", "seq"), axis=0, tiled=True)
+    store = []
+    u1, later, d_next = (
+        lax.psum(1, ("grp", "seq")),
+        lax.axis_index(("grp", "seq")),
+        handed.shape[0],
+    )
+    for dev_i, d in enumerate(handed.shape):
+        store.append(d * u1 if dev_i == 0 else d)
+    landed = lax.dynamic_update_slice_in_dim(
+        jnp.zeros(store, handed.dtype), handed, later * d_next, axis=0
+    )
+    tall = step_out = handed
+    for k0 in range(1, u1 // 2 + 1):
+        trail = []
+        for dev_i in range(u1):
+            trail.append((dev_i, (dev_i + 1) % u1))
+        tall = lax.ppermute(tall, ("grp", "seq"), trail)
+        landed = lax.dynamic_update_slice_in_dim(landed, tall, (later - k0) % u1 * d_next, axis=0)
+        if 2 * k0 < u1:
+            tray = []
+            for dev_i in range(u1):
+                tray.append((dev_i, (dev_i - 1) % u1))
+            step_out = lax.ppermute(step_out, ("grp", "seq"), tray)
+            landed = lax.dynamic_update_slice_in_dim(
+                landed, step_out, (later + k0) % u1 * d_next, axis=0
+            )
     landed = landed.reshape(total_blocks, BLOCK, row_width)
     block_ids = jnp.arange(total_blocks, dtype=jnp.int32)
     order_key = jnp.where(owners == my_owner, block_ids, total_blocks + block_ids)

time: 229 us -> 249 us (1.087)
  starting transfers between devices: 1.28 us -> 37.6 us
  waiting for transfers between devices: 30.4 us -> 17.2 us
  between operations: 13.4 us -> 0.3 us
  local copies, waits for them, and re-layouts: 94 us -> 103 us
    ppermute x0 -> x15, starting transfers between devices: none -> 36.3 us  [the longest x7 34.2 us: local(): step_out = lax.ppermute(step_out, ('grp', 'seq'), tray)]
    all_gather x1 -> x0, waiting for transfers between devices: 28.3 us -> none  [local(): landed = lax.all_gather(handed, ('grp', 'seq'), axis=0, tiled=True)]
    ppermute x0 -> x15, waiting for transfers between devices: none -> 15.1 us  [the longest x8 12.4 us: local(): tall = lax.ppermute(tall, ('grp', 'seq'), trail)]
    dynamic_update_slice x0 -> x16, local copies, waits for them, and re-layouts: none -> 11.7 us  [the longest x8 5.71 us: local(): lax.dynamic_update_slice_in_dim(landed, tall, (later - k0) % u1 * d_next,...]
  transfers between devices with their start and end apart: 2 -> 16, of which waited for: 2 -> 7; matrix products, arithmetic and copies ran while one was open for 1% -> 1% of each run, Pallas kernels for 0% -> 0%
where the time goes in v1:
time: 249 us; the launch traced here: 248 us
  local copies, waits for them, and re-layouts  103 us (41%)
  matrix products  37.7 us (15%)
  starting transfers between devices  37.6 us (15%)
  other arithmetic  27.1 us (11%)
  blocking collectives  24.7 us (10%)
  waiting for transfers between devices  17.2 us (7%)
    gather x1, local copies, waits for them, and re-layouts, decode_side(): windows = jnp.take(padded, row_index, axis=0)  72.1 us
    ppermute x7, starting transfers between devices, local(): step_out = lax.ppermute(step_out, ('grp', 'seq'), tray)  34.2 us
    select_n x1, other arithmetic, decode_side(): windows = jnp.take(padded, row_index, axis=0)  18.1 us
    dot_general x1, matrix products, decode_side(): jnp.einsum('rhw,rtw->rht', own_query, windows, preferred_element_type=jnp...  13.1 us
    all_gather x1, blocking collectives, local(): lax.all_gather(own_stream, 'seq', axis=0, tiled=True)  12.7 us
    ppermute x8, waiting for transfers between devices, local(): tall = lax.ppermute(tall, ('grp', 'seq'), trail)  12.4 us
    dot_general x1, matrix products, decode_side(): jnp.einsum('rht,rtl->rhl', weights[:, :, :MOSTLEN], windows[:, :, :LAT],...  12.1 us
    all_gather x1, blocking collectives, local(): lax.all_gather(own_span, 'seq', axis=0, tiled=True)  12.1 us
  transfers between devices with their start and end apart: 16, of which 7 were waited for; matrix products, arithmetic and copies ran while one was open for 1% of the time, Pallas kernels for 0%

profile of v1, /device:TPU:1, one launch (start us, length us, event | category | flops | bytes accessed | tf_op | source)
XLA Modules:
  0.0 248.2 jit_solution(9310816566426398019)
XLA Ops:
  1.3 2.1 collective-permute-done
  3.4 2.1 collective-permute-start.1
  5.5 3.9 %collective-permute-start.2 = (bf16[64,576]{1,0:T(8,128)(2,1)S(1)}, bf16[64,576]{1,0:T(8,128)(2,1)S(1)}, u32[]{:S(2)}, u32[]{:S(2)}) collective-permute-start(bf16[64,576]{1,0:T(8,128)(2,1)S(1)} %collective-permute-done), channel_id=1, source_target_pairs={{0,27},{1,0},{2,1},{3,2},{8,3},{9,8},{10,9},{11,10},{16,11},{17,16... | collective-permute-start | bytes 221192 | tf_op jit(solution)/shard_map/ppermute | solution.py:144
  9.4 2.7 %collective-permute-done.1 = bf16[64,576]{1,0:T(8,128)(2,1)S(1)} collective-permute-done((bf16[64,576]{1,0:T(8,128)(2,1)S(1)}, bf16[64,576]{1,0:T(8,128)(2,1)S(1)}, u32[]{:S(2)}, u32[]{:S(2)}) %collective-permute-start.1) | collective-permute-done | bytes 73760 | tf_op jit(solution)/shard_map/ppermute | solution.py:138
  12.1 5.1 %collective-permute-start.4 = (bf16[64,576]{1,0:T(8,128)(2,1)S(1)}, bf16[64,576]{1,0:T(8,128)(2,1)S(1)}, u32[]{:S(2)}, u32[]{:S(2)}) collective-permute-start(bf16[64,576]{1,0:T(8,128)(2,1)S(1)} %collective-permute-done.2), channel_id=1, source_target_pairs={{0,27},{1,0},{2,1},{3,2},{8,3},{9,8},{10,9},{11,10},{16,11},{17,16... | collective-permute-start | bytes 221192 | tf_op jit(solution)/shard_map/ppermute | solution.py:144
  19.1 5.1 %collective-permute-start.6 = (bf16[64,576]{1,0:T(8,128)(2,1)S(1)}, bf16[64,576]{1,0:T(8,128)(2,1)S(1)}, u32[]{:S(2)}, u32[]{:S(2)}) collective-permute-start(bf16[64,576]{1,0:T(8,128)(2,1)S(1)} %collective-permute-done.4), channel_id=1, source_target_pairs={{0,27},{1,0},{2,1},{3,2},{8,3},{9,8},{10,9},{11,10},{16,11},{17,16... | collective-permute-start | bytes 221192 | tf_op jit(solution)/shard_map/ppermute | solution.py:144
  28.3 5.1 %collective-permute-start.8 = (bf16[64,576]{1,0:T(8,128)(2,1)S(1)}, bf16[64,576]{1,0:T(8,128)(2,1)S(1)}, u32[]{:S(2)}, u32[]{:S(2)}) collective-permute-start(bf16[64,576]{1,0:T(8,128)(2,1)S(1)} %collective-permute-done.6), channel_id=1, source_target_pairs={{0,27},{1,0},{2,1},{3,2},{8,3},{9,8},{10,9},{11,10},{16,11},{17,16... | collective-permute-start | bytes 221192 | tf_op jit(solution)/shard_map/ppermute | solution.py:144
  34.9 5.5 %collective-permute-start.10 = (bf16[64,576]{1,0:T(8,128)(2,1)S(1)}, bf16[64,576]{1,0:T(8,128)(2,1)S(1)}, u32[]{:S(2)}, u32[]{:S(2)}) collective-permute-start(bf16[64,576]{1,0:T(8,128)(2,1)S(1)} %collective-permute-done.8), channel_id=1, source_target_pairs={{0,27},{1,0},{2,1},{3,2},{8,3},{9,8},{10,9},{11,10},{16,11},{17,16... | collective-permute-start | bytes 221192 | tf_op jit(solution)/shard_map/ppermute | solution.py:144
  40.4 12.7 %all-gather = bf16[1,1,256,576]{3,2,1,0:T(8,128)(2,1)S(1)} all-gather(bf16[1,1,64,576]{3,2,1,0:T(8,128)(2,1)} %param.12), channel_id=2, replica_groups=mesh['grp'=4,'side'=2,'seq'=4] {'seq'}, dimensions={2}, use_global_device_ids=true | all-gather | bytes 368640 | tf_op jit(solution)/shard_map/all_gather | solution.py:118
  53.1 4.9 %collective-permute-start.12 = (bf16[64,576]{1,0:T(8,128)(2,1)S(1)}, bf16[64,576]{1,0:T(8,128)(2,1)S(1)}, u32[]{:S(2)}, u32[]{:S(2)}) collective-permute-start(bf16[64,576]{1,0:T(8,128)(2,1)S(1)} %collective-permute-done.10), channel_id=1, source_target_pairs={{0,27},{1,0},{2,1},{3,2},{8,3},{9,8},{10,9},{11,10},{16,11},{17,16... | collective-permute-start | bytes 221192 | tf_op jit(solution)/shard_map/ppermute | solution.py:144
  57.9 12.1 %all-gather.1 = bf16[1,256,576]{2,1,0:T(8,128)(2,1)S(1)} all-gather(bf16[1,64,576]{2,1,0:T(8,128)(2,1)} %param.13), channel_id=3, replica_groups=mesh['grp'=4,'side'=2,'seq'=4] {'seq'}, dimensions={1}, use_global_device_ids=true | all-gather | bytes 368640 | tf_op jit(solution)/shard_map/all_gather | solution.py:119
  70.0 4.6 %collective-permute-start.14 = (bf16[64,576]{1,0:T(8,128)(2,1)S(1)}, bf16[64,576]{1,0:T(8,128)(2,1)S(1)}, u32[]{:S(2)}, u32[]{:S(2)}) collective-permute-start(bf16[64,576]{1,0:T(8,128)(2,1)S(1)} %collective-permute-done.12), channel_id=1, source_target_pairs={{0,27},{1,0},{2,1},{3,2},{8,3},{9,8},{10,9},{11,10},{16,11},{17,16... | collective-permute-start | bytes 221192 | tf_op jit(solution)/shard_map/ppermute | solution.py:144
  76.1 6.0 %collective-permute-done.15 = bf16[64,576]{1,0:T(8,128)(2,1)S(1)} collective-permute-done((bf16[64,576]{1,0:T(8,128)(2,1)S(1)}, bf16[64,576]{1,0:T(8,128)(2,1)S(1)}, u32[]{:S(2)}, u32[]{:S(2)}) %collective-permute-start.15) | collective-permute-done | bytes 73760 | tf_op jit(solution)/shard_map/ppermute | solution.py:138
  82.1 164.1 %conditional.1 = (bf16[1,1,64,64,512]{4,3,2,1,0:T(8,128)(2,1)S(1)}) conditional(s32[]{:T(128)} %convert_element_type.20, (s32[1,64]{1,0:T(1,128)}, s32[32]{0:T(128)}, bf16[4096,576]{0,1:T(8,128)(2,1)}, bf16[1,1,64,64,576]{4,3,2,1,0:T(8,128)(2,1)}, bf16[64,576]{1,0:T(8,128)(2,1)}, /*index=5*/s32[4,1]{0,1:T(1,128)S(1)}, s32[32]{0:T(128)}, ...), branch_computations={%region_1.5_spmd.clone, %region_5.10_spmd} | conditional | flops 3458017280 | bytes 202494112 | solution.py:160
  82.1 7.6 %copy.55 = bf16[4096,576]{1,0:T(8,128)(2,1)} copy(bf16[4096,576]{0,1:T(8,128)(2,1)} %get-tuple-element.740) | data formatting | bytes 9437184 | tf_op jit(solution)/shard_map
  89.7 5.4 %concatenate.14 = bf16[4352,576]{1,0:T(8,128)(2,1)} pad(bf16[4096,576]{1,0:T(8,128)(2,1)} %copy.55, bf16[]{:T(256)} %constant.137.clone.1), padding=0_256x0_0 | pad | bytes 9732098 | tf_op jit(solution)/shard_map/cond/branch_0_fun/concatenate | solution.py:58
  95.6 72.1 %gather_fusion = bf16[16384,576]{1,0:T(8,128)(2,1)} fusion(bf16[4352,576]{1,0:T(8,128)(2,1)} %concatenate.14, s32[16384]{0:T(1024)S(1)} %broadcast_clamp_fusion), kind=kCustom, calls=%fused_computation | custom fusion | bytes 37814272 | tf_op jit(solution)/shard_map/cond/branch_0_fun/jit(_take)/gather | solution.py:62
  167.8 18.1 %broadcast_select_fusion = bf16[64,256,576]{2,1,0:T(8,128)(2,1)} fusion(bf16[64,256,576]{2,1,0:T(8,128)(2,1)} %bitcast.97, pred[64,256]{1,0:T(8,128)(4,1)S(1)} %fusion.50), kind=kLoop, calls=%fused_computation.29 | loop fusion | flops 9437184 | bytes 37765120 | tf_op jit(solution)/shard_map/cond/branch_0_fun/jit(_take)/select_n | solution.py:62
  185.9 4.2 %fusion.30 = f32[64,1,64]{2,1,0:T(1,128)S(1)} fusion(bf16[1,1,64,64,576]{4,3,2,1,0:T(8,128)(2,1)} %get-tuple-element.277, bf16[64,576,1]{1,0,2:T(8,128)(2,1)S(1)} %bitcast.106), kind=kOutput, calls=%fused_computation.36 | convolution fusion | flops 4718592 | bytes 4808704 | tf_op jit(solution)/shard_map/cond/branch_0_fun/rhw,rw->rh/dot_general | solution.py:70
  204.8 4.0 %multiply_bitcast_fusion.1 = f32[64,64,128]{2,1,0:T(8,128)S(1)} fusion(bf16[128,576,1]{1,0,2:T(8,128)(2,1)S(1)} %bitcast.102, bf16[1,1,64,64,576]{4,3,2,1,0:T(8,128)(2,1)} %get-tuple-element.277), kind=kOutput, calls=%fused_computation.49 | convolution fusion | flops 604504064 | bytes 6963200 | tf_op jit(solution)/shard_map/cond/branch_0_fun/rhw,kw->rhk/dot_general | solution.py:67
  208.8 13.1 %multiply_bitcast_fusion = f32[64,64,256]{2,1,0:T(8,128)} fusion(bf16[64,256,576]{2,1,0:T(8,128)(2,1)} %broadcast_select_fusion, bf16[1,1,64,64,576]{4,3,2,1,0:T(8,128)(2,1)} %get-tuple-element.277), kind=kOutput, calls=%fused_computation.45 | convolution fusion | flops 1209008128 | bytes 27787264 | tf_op jit(solution)/shard_map/cond/branch_0_fun/rhw,rtw->rht/dot_general | solution.py:64
  223.6 4.4 %fusion.58 = (f32[64,64]{1,0:T(8,128)S(1)}, f32[64,64,385]{2,1,0:T(8,128)S(1)}) fusion(f32[64,64,1]{2,1,0:T(8,128)} %copy.51, f32[64,64,128]{2,1,0:T(8,128)S(1)} %multiply_bitcast_fusion.1, f32[64,64,256]{2,1,0:T(8,128)} %multiply_bitcast_fusion, pred[64,385]{1,0:T(8,128)(4,1)S(1)} %add_add_fusion), kind=kOutput, calls=%fused_computation.74 | output fusion | flops 7885184 | bytes 12656704 | tf_op jit(solution)/shard_map/cond/branch_0_fun/sub | solution.py:23
  229.0 12.1 %fusion.28 = f32[64,64,512]{2,1,0:T(8,128)} fusion(bf16[64,256,576]{2,1,0:T(8,128)(2,1)} %broadcast_select_fusion, bf16[64,64,385]{2,1,0:T(8,128)(2,1)S(1)} %divide_convert_fusion.2), kind=kOutput, calls=%fused_computation.30 | convolution fusion | flops 1073741824 | bytes 27262976 | tf_op jit(solution)/shard_map/cond/branch_0_fun/rht,rtl->rhl/dot_general | solution.py:82
  241.7 4.2 %fusion.37 = bf16[1,1,64,64,512]{4,3,2,1,0:T(8,128)(2,1)S(1)} fusion(f32[64,64,512]{2,1,0:T(8,128)} %fusion.28, f32[64,512]{1,0:T(8,128)S(1)} %slice_convert_fusion, f32[64,64]{1,0:T(8,128)S(1)} %convert_reduce_fusion, bf16[64,64,385]{2,1,0:T(8,128)(2,1)S(1)} %divide_convert_fusion.2, bf16[128,576]{1,0:T(8,128)(2,1)S(1)} %bitcast.103), kind=kOutput, calls=%fused_computation.43 | convolution fusion | flops 545259520 | bytes 13926400 | tf_op jit(solution)/shard_map/cond/branch_0_fun/rhk,kl->rhl/dot_general | solution.py:88
  (78 shorter events, 30.3 us)
Async XLA Ops:
  0.0 3.4 %collective-permute-start = (bf16[64,576]{1,0:T(8,128)(2,1)}, bf16[64,576]{1,0:T(8,128)(2,1)S(1)}, u32[]{:S(2)}, u32[]{:S(2)}) collective-permute-start(bf16[64,576]{1,0:T(8,128)(2,1)} %bitcast.104), channel_id=1, source_target_pairs={{0,4},{1,5},{2,6},{3,7},{8,12},{9,13},{10,14},{11,15},{16,20},{17,... | collective-permute-start | bytes 221192 | tf_op jit(solution)/shard_map/ppermute | solution.py:17
  3.4 8.7 %collective-permute-start.1 = (bf16[64,576]{1,0:T(8,128)(2,1)S(1)}, bf16[64,576]{1,0:T(8,128)(2,1)S(1)}, u32[]{:S(2)}, u32[]{:S(2)}) collective-permute-start(bf16[64,576]{1,0:T(8,128)(2,1)S(1)} %collective-permute-done), channel_id=1, source_target_pairs={{0,1},{1,2},{2,3},{3,8},{8,9},{9,10},{10,11},{11,16},{16,17},{17,1... | collective-permute-start | bytes 221192 | tf_op jit(solution)/shard_map/ppermute | solution.py:138
  5.5 6.6 %collective-permute-start.2 = (bf16[64,576]{1,0:T(8,128)(2,1)S(1)}, bf16[64,576]{1,0:T(8,128)(2,1)S(1)}, u32[]{:S(2)}, u32[]{:S(2)}) collective-permute-start(bf16[64,576]{1,0:T(8,128)(2,1)S(1)} %collective-permute-done), channel_id=1, source_target_pairs={{0,27},{1,0},{2,1},{3,2},{8,3},{9,8},{10,9},{11,10},{16,11},{17,16... | collective-permute-start | bytes 221192 | tf_op jit(solution)/shard_map/ppermute | solution.py:144
  12.1 7.0 %collective-permute-start.3 = (bf16[64,576]{1,0:T(8,128)(2,1)S(1)}, bf16[64,576]{1,0:T(8,128)(2,1)S(1)}, u32[]{:S(2)}, u32[]{:S(2)}) collective-permute-start(bf16[64,576]{1,0:T(8,128)(2,1)S(1)} %collective-permute-done.1), channel_id=1, source_target_pairs={{0,1},{1,2},{2,3},{3,8},{8,9},{9,10},{10,11},{11,16},{16,17},{17,1... | collective-permute-start | bytes 221192 | tf_op jit(solution)/shard_map/ppermute | solution.py:138
  12.1 7.0 %collective-permute-start.4 = (bf16[64,576]{1,0:T(8,128)(2,1)S(1)}, bf16[64,576]{1,0:T(8,128)(2,1)S(1)}, u32[]{:S(2)}, u32[]{:S(2)}) collective-permute-start(bf16[64,576]{1,0:T(8,128)(2,1)S(1)} %collective-permute-done.2), channel_id=1, source_target_pairs={{0,27},{1,0},{2,1},{3,2},{8,3},{9,8},{10,9},{11,10},{16,11},{17,16... | collective-permute-start | bytes 221192 | tf_op jit(solution)/shard_map/ppermute | solution.py:144
  19.0 7.0 %collective-permute-start.5 = (bf16[64,576]{1,0:T(8,128)(2,1)S(1)}, bf16[64,576]{1,0:T(8,128)(2,1)S(1)}, u32[]{:S(2)}, u32[]{:S(2)}) collective-permute-start(bf16[64,576]{1,0:T(8,128)(2,1)S(1)} %collective-permute-done.3), channel_id=1, source_target_pairs={{0,1},{1,2},{2,3},{3,8},{8,9},{9,10},{10,11},{11,16},{16,17},{17,1... | collective-permute-start | bytes 221192 | tf_op jit(solution)/shard_map/ppermute | solution.py:138
  19.1 9.3 %collective-permute-start.6 = (bf16[64,576]{1,0:T(8,128)(2,1)S(1)}, bf16[64,576]{1,0:T(8,128)(2,1)S(1)}, u32[]{:S(2)}, u32[]{:S(2)}) collective-permute-start(bf16[64,576]{1,0:T(8,128)(2,1)S(1)} %collective-permute-done.4), channel_id=1, source_target_pairs={{0,27},{1,0},{2,1},{3,2},{8,3},{9,8},{10,9},{11,10},{16,11},{17,16... | collective-permute-start | bytes 221192 | tf_op jit(solution)/shard_map/ppermute | solution.py:144
  26.0 7.3 %collective-permute-start.7 = (bf16[64,576]{1,0:T(8,128)(2,1)S(1)}, bf16[64,576]{1,0:T(8,128)(2,1)S(1)}, u32[]{:S(2)}, u32[]{:S(2)}) collective-permute-start(bf16[64,576]{1,0:T(8,128)(2,1)S(1)} %collective-permute-done.5), channel_id=1, source_target_pairs={{0,1},{1,2},{2,3},{3,8},{8,9},{9,10},{10,11},{11,16},{16,17},{17,1... | collective-permute-start | bytes 221192 | tf_op jit(solution)/shard_map/ppermute | solution.py:138
  28.3 6.5 %collective-permute-start.8 = (bf16[64,576]{1,0:T(8,128)(2,1)S(1)}, bf16[64,576]{1,0:T(8,128)(2,1)S(1)}, u32[]{:S(2)}, u32[]{:S(2)}) collective-permute-start(bf16[64,576]{1,0:T(8,128)(2,1)S(1)} %collective-permute-done.6), channel_id=1, source_target_pairs={{0,27},{1,0},{2,1},{3,2},{8,3},{9,8},{10,9},{11,10},{16,11},{17,16... | collective-permute-start | bytes 221192 | tf_op jit(solution)/shard_map/ppermute | solution.py:144
  33.4 7.0 %collective-permute-start.9 = (bf16[64,576]{1,0:T(8,128)(2,1)S(1)}, bf16[64,576]{1,0:T(8,128)(2,1)S(1)}, u32[]{:S(2)}, u32[]{:S(2)}) collective-permute-start(bf16[64,576]{1,0:T(8,128)(2,1)S(1)} %collective-permute-done.7), channel_id=1, source_target_pairs={{0,1},{1,2},{2,3},{3,8},{8,9},{9,10},{10,11},{11,16},{16,17},{17,1... | collective-permute-start | bytes 221192 | tf_op jit(solution)/shard_map/ppermute | solution.py:138
  34.9 18.2 %collective-permute-start.10 = (bf16[64,576]{1,0:T(8,128)(2,1)S(1)}, bf16[64,576]{1,0:T(8,128)(2,1)S(1)}, u32[]{:S(2)}, u32[]{:S(2)}) collective-permute-start(bf16[64,576]{1,0:T(8,128)(2,1)S(1)} %collective-permute-done.8), channel_id=1, source_target_pairs={{0,27},{1,0},{2,1},{3,2},{8,3},{9,8},{10,9},{11,10},{16,11},{17,16... | collective-permute-start | bytes 221192 | tf_op jit(solution)/shard_map/ppermute | solution.py:144
  40.4 17.5 %collective-permute-start.11 = (bf16[64,576]{1,0:T(8,128)(2,1)S(1)}, bf16[64,576]{1,0:T(8,128)(2,1)S(1)}, u32[]{:S(2)}, u32[]{:S(2)}) collective-permute-start(bf16[64,576]{1,0:T(8,128)(2,1)S(1)} %collective-permute-done.9), channel_id=1, source_target_pairs={{0,1},{1,2},{2,3},{3,8},{8,9},{9,10},{10,11},{11,16},{16,17},{17,1... | collective-permute-start | bytes 221192 | tf_op jit(solution)/shard_map/ppermute | solution.py:138
  53.1 16.9 %collective-permute-start.12 = (bf16[64,576]{1,0:T(8,128)(2,1)S(1)}, bf16[64,576]{1,0:T(8,128)(2,1)S(1)}, u32[]{:S(2)}, u32[]{:S(2)}) collective-permute-start(bf16[64,576]{1,0:T(8,128)(2,1)S(1)} %collective-permute-done.10), channel_id=1, source_target_pairs={{0,27},{1,0},{2,1},{3,2},{8,3},{9,8},{10,9},{11,10},{16,11},{17,16... | collective-permute-start | bytes 221192 | tf_op jit(solution)/shard_map/ppermute | solution.py:144
  57.9 16.7 %collective-permute-start.13 = (bf16[64,576]{1,0:T(8,128)(2,1)S(1)}, bf16[64,576]{1,0:T(8,128)(2,1)S(1)}, u32[]{:S(2)}, u32[]{:S(2)}) collective-permute-start(bf16[64,576]{1,0:T(8,128)(2,1)S(1)} %collective-permute-done.11), channel_id=1, source_target_pairs={{0,1},{1,2},{2,3},{3,8},{8,9},{9,10},{10,11},{11,16},{16,17},{17,1... | collective-permute-start | bytes 221192 | tf_op jit(solution)/shard_map/ppermute | solution.py:138
  70.0 6.1 %collective-permute-start.14 = (bf16[64,576]{1,0:T(8,128)(2,1)S(1)}, bf16[64,576]{1,0:T(8,128)(2,1)S(1)}, u32[]{:S(2)}, u32[]{:S(2)}) collective-permute-start(bf16[64,576]{1,0:T(8,128)(2,1)S(1)} %collective-permute-done.12), channel_id=1, source_target_pairs={{0,27},{1,0},{2,1},{3,2},{8,3},{9,8},{10,9},{11,10},{16,11},{17,16... | collective-permute-start | bytes 221192 | tf_op jit(solution)/shard_map/ppermute | solution.py:144
  74.6 7.5 %collective-permute-start.15 = (bf16[64,576]{1,0:T(8,128)(2,1)S(1)}, bf16[64,576]{1,0:T(8,128)(2,1)S(1)}, u32[]{:S(2)}, u32[]{:S(2)}) collective-permute-start(bf16[64,576]{1,0:T(8,128)(2,1)S(1)} %collective-permute-done.13), channel_id=1, source_target_pairs={{0,1},{1,2},{2,3},{3,8},{8,9},{9,10},{10,11},{11,16},{16,17},{17,1... | collective-permute-start | bytes 221192 | tf_op jit(solution)/shard_map/ppermute | solution.py:138
  89.7 5.4 %copy-start.4 = (s32[1,64]{1,0:T(1,128)S(1)}, s32[1,64]{1,0:T(1,128)}, u32[]{:S(2)}) copy-start(s32[1,64]{1,0:T(1,128)} %get-tuple-element.278) | copy-start | bytes 772 | tf_op jit(solution)/shard_map/cond
  167.8 18.2 %copy-start.3 = (bf16[64,576]{1,0:T(8,128)(2,1)S(1)}, bf16[64,576]{1,0:T(8,128)(2,1)}, u32[]{:S(2)}) copy-start(bf16[64,576]{1,0:T(8,128)(2,1)} %get-tuple-element.276) | copy-start | bytes 221188 | tf_op jit(solution)/shard_map/cond
  208.8 13.1 %copy-start.1 = (s32[32]{0:T(128)S(1)}, s32[32]{0:T(128)}, u32[]{:S(2)}) copy-start(s32[32]{0:T(128)} %get-tuple-element.305) | copy-start | bytes 388 | tf_op jit(solution)/shard_map/cond
  208.8 13.8 %copy-start = (s32[32]{0:T(128)S(1)}, s32[32]{0:T(128)}, u32[]{:S(2)}) copy-start(s32[32]{0:T(128)} %get-tuple-element.287) | copy-start | bytes 388 | tf_op jit(solution)/shard_map/cond
  246.2 2.0 copy-start.2
